TPU v7x, 256 devices: a whole 4x4x8 slice. The times are simulated.
256 devices in a mesh: tm: 64 (over z, y, core), site: 4 (over x).
Axes of the slice: x: 4, y: 4, z: 8, core: 2. Of those that a mesh axis runs over, the one named last changes fastest.
Arguments:
- obs_rows: bfloat16 [131072, 256], P(('tm', 'site')), may hold values from -2 to 2
- obs_values: bfloat16 [131072], P(('tm', 'site')), may hold values from -6 to 6
- obs_hours: int32 [131072], P(('tm', 'site')), may hold values from 0 to 3
- prior_precision: float32 [256, 256], replicated, may hold values from -1 to 3, as said below
- transition: float32 [256, 256], replicated, may hold values from -1 to 1
- site_basis: bfloat16 [1048576, 256], P(('tm', 'site')), may hold values from -0.375 to 0.375
Outputs:
- prediction: bfloat16 [256, 1048576], P(None, ('tm', 'site'))
Inputs may be any that keep to these rules, and one draw needn't show every extreme that they name: `prior_precision`: symmetric and positive definite.
All inputs are finite; a program needn't handle non-finite values. Where the computation divides by a largest or mean magnitude, that divisor is 1e-20 or more.
Results may differ from a plain program's by a relative error of at most 0.0049.
Values may be sent and summed in bfloat16 or wider, within the bound.
A program may use at most 64 MiB of HBM per device.

v0:
```python
import jax
import jax.numpy as jnp
from jax import lax
from jax.sharding import PartitionSpec as P

NS_ITERS = 8


def entering(part, axis, combine, identity):
    place = lax.axis_index(axis)
    gathered = jax.tree.map(lambda a: lax.all_gather(a, axis), part)
    state = jax.tree.map(lambda a, e: jnp.zeros_like(a) + jnp.asarray(e, a.dtype), part, identity)

    def one(turn, state):
        return combine(
            state, jax.tree.map(lambda a: lax.dynamic_index_in_dim(a, turn, 0, False), gathered)
        )

    return lax.fori_loop(0, place, one, state)


def approx_inverse(precisions):
    states = precisions.shape[-1]
    bounds = jnp.max(jnp.sum(jnp.abs(precisions), axis=2), axis=1)
    identity = jnp.eye(states, dtype=jnp.float32)
    inverse = identity[None] / bounds[:, None, None]
    for iteration in range(NS_ITERS):
        product = jnp.einsum("hij,hjk->hik", precisions, inverse, precision=lax.Precision.HIGHEST)
        inverse = jnp.einsum(
            "hij,hjk->hik", inverse, 2.0 * identity - product, precision=lax.Precision.HIGHEST
        )
    return inverse


def compose(earlier, latter):
    joined_map = jnp.dot(latter[0], earlier[0], precision=lax.Precision.HIGHEST)
    joined_shift = jnp.dot(latter[0], earlier[1], precision=lax.Precision.HIGHEST) + latter[1]
    return (joined_map, joined_shift)


def hour_elements(summed_grams, drives, prior_precision, coupled):
    inverse = approx_inverse(prior_precision[None] + summed_grams)
    hour_maps = jnp.einsum("hij,jk->hik", inverse, coupled, precision=lax.Precision.HIGHEST)
    offsets = jnp.einsum("hij,hj->hi", inverse, drives, precision=lax.Precision.HIGHEST)
    return (hour_maps, offsets)


def body(obs_rows, obs_values, obs_hours, prior_precision, transition, site_basis):
    blocks = lax.axis_size("site")
    row_count = obs_rows.shape[0]
    hour_slot = lax.broadcasted_iota(jnp.int32, (blocks, row_count), 0)
    member = obs_hours[None, :] == hour_slot
    masked = jnp.where(member[:, :, None], obs_rows[None], jnp.zeros((), jnp.bfloat16))
    local_grams = jnp.einsum("hrs,rt->hst", masked, obs_rows, preferred_element_type=jnp.float32)
    weighted = jnp.where(member, obs_values[None], jnp.zeros((), jnp.bfloat16))
    local_drives = jnp.einsum("hr,rs->hs", weighted, obs_rows, preferred_element_type=jnp.float32)
    summed_grams, drives = (
        lax.psum_scatter(local_grams, "site", scatter_dimension=0, tiled=True),
        lax.psum_scatter(local_drives, "site", scatter_dimension=0, tiled=True),
    )
    coupled = jnp.dot(prior_precision, transition, precision=lax.Precision.HIGHEST)
    states = transition.shape[0]
    identity = jnp.eye(states, dtype=jnp.float32)
    zero_state = jnp.zeros((states,), jnp.float32)
    hour_maps, offsets = hour_elements(summed_grams, drives, prior_precision, coupled)
    block_maps, block_offsets = (
        lax.all_gather(hour_maps, "site", axis=0, tiled=True),
        lax.all_gather(offsets, "site", axis=0, tiled=True),
    )
    joined = (block_maps[0], block_offsets[0])
    for position in range(1, blocks):
        joined = compose(joined, (block_maps[position], block_offsets[position]))
    before = entering(joined, "tm", compose, (identity, zero_state))
    state_mean = before[1]
    results = []
    for position in range(blocks):
        state_mean = (
            jnp.dot(block_maps[position], state_mean, precision=lax.Precision.HIGHEST)
            + block_offsets[position]
        )
        results.append(state_mean)
    rounded = jnp.stack(results).astype(jnp.bfloat16)
    return jnp.einsum(
        "hs,ns->hn",
        lax.all_gather(rounded, "tm", axis=0, tiled=True),
        site_basis,
        preferred_element_type=jnp.float32,
    ).astype(jnp.bfloat16)


def solution(mesh):
    in_specs = (
        P(("tm", "site"), None),
        P(("tm", "site")),
        P(("tm", "site")),
        P(),
        P(),
        P(("tm", "site"), None),
    )
    out_specs = P(None, ("tm", "site"))
    return jax.shard_map(body, mesh=mesh, in_specs=in_specs, out_specs=out_specs, check_vma=False)
```

profile of v0, /device:TPU:1, one launch (start us, length us, event | category | flops | bytes accessed | tf_op | source)
XLA Modules:
  0.0 322.2 jit_solution(5100696245763074373)
XLA Ops:
  6.5 1.2 copy.8
  7.8 0.7 iota_compare_fusion.3
  8.5 2.4 fusion.4
  11.3 28.3 %reduce-scatter.2.cloned.1.call-done = f32[1,256,256]{2,1,0:T(8,128)} async-done(((f32[4,256,256]{2,1,0:T(8,128)}), f32[1,256,256]{2,1,0:T(8,128)}) %reduce-scatter.2.cloned.1.call-update) | async-done | bytes 262160 | tf_op jit(solution)/shard_map/reduce_scatter | solution.py:58
  39.6 1.1 abs_reduce_fusion
  40.7 0.6 reduce_max.9
  42.7 0.4 convolution_subtract_fusion.6
  43.5 0.4 convolution_subtract_fusion.5
  48.2 1.1 fusion.69
  49.4 26.0 %all-gather.10.cloned.1.call-done = f32[1024,256]{1,0:T(8,128)} async-done(((f32[256,256]{1,0:T(8,128)}), f32[1024,256]{1,0:T(8,128)}) %all-gather.10.cloned.1.call-update) | async-done | bytes 1048592 | tf_op jit(solution)/shard_map/all_gather | solution.py:67
  75.3 1.5 fusion.21
  76.8 1.3 fusion.32
  78.2 2.0 fusion.38
  80.2 0.6 dynamic-slice
  80.8 1.1 fusion.46
  81.9 7.7 %all-reduce = f32[4,256]{1,0:T(4,128)S(1)} all-reduce(f32[4,256]{1,0:T(4,128)S(1)} %fusion.46), channel_id=7, replica_groups=mesh['tm'=64,'site'=4] {'site'}, use_global_device_ids=true, to_apply=%region_3.4.clone | all-reduce | flops 1024 | bytes 8192
  89.6 0.9 convolution_bitcast_fusion
  90.5 5.3 %all-gather.4 = f32[4,1,256]{2,1,0:T(1,128)S(1)} all-gather(f32[1,1,256]{2,1,0:T(1,128)S(1)} %convolution_bitcast_fusion), channel_id=4, replica_groups=mesh['tm'=64,'site'=4] {'site'}, dimensions={0}, use_global_device_ids=true | all-gather | bytes 5120 | tf_op jit(solution)/shard_map/all_gather | solution.py:68
  96.8 51.4 %all-gather.5 = f32[64,1,256]{2,1,0:T(1,128)S(1)} all-gather(f32[1,1,256]{2,1,0:T(1,128)S(1)} %bitcast.138), channel_id=5, replica_groups=mesh['tm'=64,'site'=4] {'tm'}, dimensions={0}, use_global_device_ids=true | all-gather | bytes 66560 | tf_op jit(solution)/shard_map/all_gather | solution.py:11
  148.1 34.4 %all-gather.12.cloned.1.call-done = f32[16384,256]{1,0:T(8,128)} async-done(((f32[256,256]{1,0:T(8,128)}), f32[16384,256]{1,0:T(8,128)}) %all-gather.12.cloned.1.call-update) | async-done | bytes 16777232 | tf_op jit(solution)/shard_map/all_gather | solution.py:11
  182.5 1.3 while.12
  182.5 1.2 fusion.114
  185.2 128.3 %all-gather.6 = bf16[64,4,256]{2,1,0:T(4,128)(2,1)S(1)} all-gather(bf16[1,4,256]{2,1,0:T(4,128)(2,1)S(1)} %maximum_bitcast_fusion), channel_id=1, replica_groups=mesh['tm'=64,'site'=4] {'tm'}, dimensions={0}, use_global_device_ids=true | all-gather | bytes 133120 | tf_op jit(solution)/shard_map/all_gather | solution.py:85
  313.6 2.1 convolution_convert_fusion
  (60 shorter events, 8.1 us)
Async XLA Ops:
  6.5 307.1 %copy-start = (bf16[4096,256]{1,0:T(8,128)(2,1)S(1)}, bf16[4096,256]{1,0:T(8,128)(2,1)}, u32[]{:S(2)}) copy-start(bf16[4096,256]{1,0:T(8,128)(2,1)} %param.13) | copy-start | bytes 6291460
  6.5 4.4 %copy-start.2 = (f32[256,256]{1,0:T(8,128)S(1)}, f32[256,256]{1,0:T(8,128)}, u32[]{:S(2)}) copy-start(f32[256,256]{1,0:T(8,128)} %param.11) | copy-start | bytes 786436
  6.5 4.4 %copy-start.3 = (f32[256,256]{1,0:T(8,128)S(1)}, f32[256,256]{1,0:T(8,128)}, u32[]{:S(2)}) copy-start(f32[256,256]{1,0:T(8,128)} %param.12) | copy-start | bytes 786436
  6.5 33.1 %reduce-scatter.2.cloned.1.call-start = ((), (), s32[]{:S(2)}) async-start(), calls=%async_computation.1 | async-start | bytes 1310720 | tf_op jit(solution)/shard_map/reduce_scatter | solution.py:58
  10.9 64.4 %all-gather.10.cloned.1.call-start = ((), (), s32[]{:S(2)}) async-start(), calls=%async_computation.2 | async-start | bytes 1310720 | tf_op jit(solution)/shard_map/all_gather | solution.py:67
  47.8 32.4 %copy-start.6 = (u32[256]{0:T(256)S(1)}, u32[256]{0:T(256)}, u32[]{:S(2)}) copy-start(u32[256]{0:T(256)} %constant.40) | copy-start | bytes 3076
  47.8 33.0 %copy-start.4 = (s32[512]{0:T(512)S(1)}, s32[512]{0:T(512)}, u32[]{:S(2)}) copy-start(s32[512]{0:T(512)} %param.10) | copy-start | bytes 6148
  47.8 33.0 %copy-start.5 = (bf16[512]{0:T(512)(128)(2,1)S(1)}, bf16[512]{0:T(512)(128)(2,1)}, u32[]{:S(2)}) copy-start(bf16[512]{0:T(512)(128)(2,1)} %param.9) | copy-start | bytes 3076
  49.3 133.2 %all-gather.12.cloned.1.call-start = ((), (), s32[]{:S(2)}) async-start(), calls=%async_computation.3 | async-start | bytes 17039360 | tf_op jit(solution)/shard_map/all_gather | solution.py:11
  75.3 20.5 %copy-start.1 = (f32[1024,256]{1,0:T(8,128)S(1)}, f32[1024,256]{1,0:T(8,128)}, u32[]{:S(2)}) copy-start(f32[1024,256]{1,0:T(8,128)} %all-gather.10.cloned.1.call-done) | copy-start | bytes 3145732
Sparse Core Ops, SparseCore 0:
  11.0 28.5 reduce-scatter.1
  49.4 25.8 all-gather.9
  80.3 102.1 all-gather.11
where the time goes:
time: 325 us; the launch traced here: 322 us
  blocking collectives  193 us (59%)
  waiting for transfers between devices  88.7 us (27%)
  matrix products  22.1 us (7%)
  between operations  14.3 us (4%)
    all_gather x1, blocking collectives, body(): lax.all_gather(rounded, 'tm', axis=0, tiled=True)  128 us
    all_gather x1, blocking collectives, entering(): gathered = jax.tree.map(lambda a: lax.all_gather(a, axis), part)  51.4 us
    all_gather x1, waiting for transfers between devices, entering(): gathered = jax.tree.map(lambda a: lax.all_gather(a, axis), part)  34.4 us
    reduce_scatter x1, waiting for transfers between devices, body(): lax.psum_scatter(local_grams, 'site', scatter_dimension=0, tiled=True)  28.3 us
    all_gather x1, waiting for transfers between devices, body(): lax.all_gather(hour_maps, 'site', axis=0, tiled=True)  26 us
    unnamed x1, blocking collectives  7.69 us
  transfers between devices with their start and end apart: 3, of which 3 were waited for; matrix products, arithmetic and copies ran while one was open for 1% of the time, Pallas kernels for 0%

commit v1 on v0

--- a/solution.py
+++ b/solution.py
@@ -4,6 +4,11 @@
 from jax.sharding import PartitionSpec as P
 
 NS_ITERS = 8
+
+
+def gather_over(x, axis, d):
+    sent = jnp.stack([x] * lax.axis_size(axis))
+    return jnp.concatenate(lax.all_to_all(sent, axis, 0, 0), axis=d)
 
 
 def entering(part, axis, combine, identity):
@@ -81,10 +86,7 @@
         results.append(state_mean)
     rounded = jnp.stack(results).astype(jnp.bfloat16)
     return jnp.einsum(
-        "hs,ns->hn",
-        lax.all_gather(rounded, "tm", axis=0, tiled=True),
-        site_basis,
-        preferred_element_type=jnp.float32,
+        "hs,ns->hn", gather_over(rounded, "tm", 0), site_basis, preferred_element_type=jnp.float32
     ).astype(jnp.bfloat16)
 
 

time: 325 us -> 293 us (0.902)
  blocking collectives: 193 us -> 161 us
    all_gather x1 -> x0, blocking collectives: 128 us -> none  [body(): lax.all_gather(rounded, 'tm', axis=0, tiled=True)]
    all_to_all x0 -> x1, blocking collectives: none -> 96.9 us  [gather_over(): return jnp.concatenate(lax.all_to_all(sent, axis, 0, 0), axis=d)]
where the time goes in v1:
time: 293 us; the launch traced here: 291 us
  blocking collectives  161 us (55%)
  waiting for transfers between devices  88.7 us (30%)
  matrix products  22 us (8%)
  between operations  14.3 us (5%)
    all_to_all x1, blocking collectives, gather_over(): return jnp.concatenate(lax.all_to_all(sent, axis, 0, 0), axis=d)  96.9 us
    all_gather x1, blocking collectives, entering(): gathered = jax.tree.map(lambda a: lax.all_gather(a, axis), part)  51.4 us
    all_gather x1, waiting for transfers between devices, entering(): gathered = jax.tree.map(lambda a: lax.all_gather(a, axis), part)  34.4 us
    reduce_scatter x1, waiting for transfers between devices, body(): lax.psum_scatter(local_grams, 'site', scatter_dimension=0, tiled=True)  28.3 us
    all_gather x1, waiting for transfers between devices, body(): lax.all_gather(hour_maps, 'site', axis=0, tiled=True)  26 us
    unnamed x1, blocking collectives  7.69 us
  transfers between devices with their start and end apart: 3, of which 3 were waited for; matrix products, arithmetic and copies ran while one was open for 1% of the time, Pallas kernels for 0%

profile of v1, /device:TPU:1, one launch (start us, length us, event | category | flops | bytes accessed | tf_op | source)
XLA Modules:
  0.0 290.8 jit_solution(5114779029206567688)
XLA Ops:
  6.5 1.2 copy.8
  7.8 0.7 iota_compare_fusion.3
  8.5 2.4 fusion.4
  11.3 28.3 %reduce-scatter.2.cloned.1.call-done = f32[1,256,256]{2,1,0:T(8,128)} async-done(((f32[4,256,256]{2,1,0:T(8,128)}), f32[1,256,256]{2,1,0:T(8,128)}) %reduce-scatter.2.cloned.1.call-update) | async-done | bytes 262160 | tf_op jit(solution)/shard_map/reduce_scatter | solution.py:63
  39.6 1.1 abs_reduce_fusion
  40.7 0.6 reduce_max.9
  45.1 0.4 convolution_subtract_fusion.3
  46.6 0.4 convolution_subtract_fusion.1
  48.2 1.1 fusion.69
  49.4 26.0 %all-gather.9.cloned.1.call-done = f32[1024,256]{1,0:T(8,128)} async-done(((f32[256,256]{1,0:T(8,128)}), f32[1024,256]{1,0:T(8,128)}) %all-gather.9.cloned.1.call-update) | async-done | bytes 1048592 | tf_op jit(solution)/shard_map/all_gather | solution.py:72
  75.3 1.5 fusion.21
  76.8 1.3 fusion.32
  78.2 2.0 fusion.38
  80.2 0.6 dynamic-slice
  80.8 1.1 fusion.46
  81.9 7.7 %all-reduce = f32[4,256]{1,0:T(4,128)S(1)} all-reduce(f32[4,256]{1,0:T(4,128)S(1)} %fusion.46), channel_id=7, replica_groups=mesh['tm'=64,'site'=4] {'site'}, use_global_device_ids=true, to_apply=%region_3.4.clone | all-reduce | flops 1024 | bytes 8192
  89.6 0.9 convolution_bitcast_fusion
  90.5 5.3 %all-gather.4 = f32[4,1,256]{2,1,0:T(1,128)S(1)} all-gather(f32[1,1,256]{2,1,0:T(1,128)S(1)} %convolution_bitcast_fusion), channel_id=4, replica_groups=mesh['tm'=64,'site'=4] {'site'}, dimensions={0}, use_global_device_ids=true | all-gather | bytes 5120 | tf_op jit(solution)/shard_map/all_gather | solution.py:73
  96.8 51.4 %all-gather.5 = f32[64,1,256]{2,1,0:T(1,128)S(1)} all-gather(f32[1,1,256]{2,1,0:T(1,128)S(1)} %bitcast.136), channel_id=5, replica_groups=mesh['tm'=64,'site'=4] {'tm'}, dimensions={0}, use_global_device_ids=true | all-gather | bytes 66560 | tf_op jit(solution)/shard_map/all_gather | solution.py:16
  148.1 34.4 %all-gather.11.cloned.1.call-done = f32[16384,256]{1,0:T(8,128)} async-done(((f32[256,256]{1,0:T(8,128)}), f32[16384,256]{1,0:T(8,128)}) %all-gather.11.cloned.1.call-update) | async-done | bytes 16777232 | tf_op jit(solution)/shard_map/all_gather | solution.py:16
  182.5 1.3 while.12
  182.5 1.2 fusion.114
  185.3 96.9 %all_to_all.5 = bf16[64,4,256]{2,1,0:T(4,128)(2,1)S(1)} all-to-all(bf16[64,4,256]{2,1,0:T(4,128)(2,1)S(1)} %stack.17), channel_id=1, replica_groups=mesh['tm'=64,'site'=4] {'tm'}, dimensions={0} | all-to-all | bytes 262144 | tf_op jit(solution)/shard_map/all_to_all | solution.py:11
  282.2 2.1 convolution_convert_fusion
  (61 shorter events, 8.1 us)
Async XLA Ops:
  6.5 275.7 %copy-start = (bf16[4096,256]{1,0:T(8,128)(2,1)S(1)}, bf16[4096,256]{1,0:T(8,128)(2,1)}, u32[]{:S(2)}) copy-start(bf16[4096,256]{1,0:T(8,128)(2,1)} %param.13) | copy-start | bytes 6291460
  6.5 4.4 %copy-start.2 = (f32[256,256]{1,0:T(8,128)S(1)}, f32[256,256]{1,0:T(8,128)}, u32[]{:S(2)}) copy-start(f32[256,256]{1,0:T(8,128)} %param.11) | copy-start | bytes 786436
  6.5 4.4 %copy-start.3 = (f32[256,256]{1,0:T(8,128)S(1)}, f32[256,256]{1,0:T(8,128)}, u32[]{:S(2)}) copy-start(f32[256,256]{1,0:T(8,128)} %param.12) | copy-start | bytes 786436
  6.5 33.1 %reduce-scatter.2.cloned.1.call-start = ((), (), s32[]{:S(2)}) async-start(), calls=%async_computation.2 | async-start | bytes 1310720 | tf_op jit(solution)/shard_map/reduce_scatter | solution.py:63
  10.9 64.4 %all-gather.9.cloned.1.call-start = ((), (), s32[]{:S(2)}) async-start(), calls=%async_computation.3 | async-start | bytes 1310720 | tf_op jit(solution)/shard_map/all_gather | solution.py:72
  47.8 32.4 %copy-start.6 = (u32[256]{0:T(256)S(1)}, u32[256]{0:T(256)}, u32[]{:S(2)}) copy-start(u32[256]{0:T(256)} %constant.40) | copy-start | bytes 3076
  47.8 33.0 %copy-start.4 = (s32[512]{0:T(512)S(1)}, s32[512]{0:T(512)}, u32[]{:S(2)}) copy-start(s32[512]{0:T(512)} %param.10) | copy-start | bytes 6148
  47.8 33.0 %copy-start.5 = (bf16[512]{0:T(512)(128)(2,1)S(1)}, bf16[512]{0:T(512)(128)(2,1)}, u32[]{:S(2)}) copy-start(bf16[512]{0:T(512)(128)(2,1)} %param.9) | copy-start | bytes 3076
  49.3 133.2 %all-gather.11.cloned.1.call-start = ((), (), s32[]{:S(2)}) async-start(), calls=%async_computation.4 | async-start | bytes 17039360 | tf_op jit(solution)/shard_map/all_gather | solution.py:16
  75.3 20.5 %copy-start.1 = (f32[1024,256]{1,0:T(8,128)S(1)}, f32[1024,256]{1,0:T(8,128)}, u32[]{:S(2)}) copy-start(f32[1024,256]{1,0:T(8,128)} %all-gather.9.cloned.1.call-done) | copy-start | bytes 3145732
Sparse Core Ops, SparseCore 0:
  11.0 28.5 reduce-scatter.1
  49.4 25.8 all-gather.8
  80.3 102.1 all-gather.10
